TPU v7x, 32 devices: a whole 2x2x4 slice. The times are simulated.
32 devices in a mesh: ep: 16 (over z, y, core), dp: 2 (over x).
Axes of the slice: x: 2, y: 2, z: 4, core: 2. Of those that a mesh axis runs over, the one named last changes fastest.
Arguments:
- hidden: bfloat16 [2, 1024, 2048], P(None, ('ep', 'dp')), may hold values from -6 to 6
- norm_gain: bfloat16 [2048], replicated, may hold values from 0.5 to 1.5
- gate_weights: float32 [2, 1024, 8], P(None, ('ep', 'dp')), may hold values from 0.05 to 1
- routes: int32 [2, 1024, 8], P(None, ('ep', 'dp')), may hold values from 0 to 15, as said below
- replica_pick: int32 [2, 1024, 8], P(None, ('ep', 'dp')), may hold values from 0 to 1023
- trainer_experts: int32 [16], replicated, may hold values from 0 to 15, each once
- hot_experts: int32 [3], replicated, may hold values from 0 to 15, as said below
- replica_hot: int32 [16], replicated, may hold values from 0 to 2, as said below
- w_gate: bfloat16 [16, 2048, 384], P('ep', 'dp'), may hold values from -0.125 to 0.125
- w_up: bfloat16 [16, 2048, 384], P('ep', 'dp'), may hold values from -0.125 to 0.125
- w_down: bfloat16 [16, 384, 2048], P('ep', None, 'dp'), may hold values from -0.3125 to 0.3125
- queries: bfloat16 [2, 1024, 4096], P(None, ('ep', 'dp')), may hold values from -6 to 6
- key_cache: bfloat16 [1024, 32, 512], P(('ep', 'dp')), may hold values from -6 to 6
- value_cache: bfloat16 [1024, 32, 512], P(('ep', 'dp')), may hold values from -6 to 6
- new_keys: bfloat16 [2, 1024, 512], P(None, ('ep', 'dp')), may hold values from -6 to 6
- new_values: bfloat16 [2, 1024, 512], P(None, ('ep', 'dp')), may hold values from -6 to 6
- cache_lengths: int32 [1024], P(('ep', 'dp')), may hold values from 2 to 32, as said below
Outputs:
- mixed: bfloat16 [2, 1024, 2048], P(None, ('ep', 'dp'))
- context: bfloat16 [2, 1024, 4096], P(None, ('ep', 'dp'))
Inputs may be any that keep to these rules, and one draw needn't show every extreme that they name: Trainer index p holds expert trainer_experts[p]; each expert once. `hot_experts`: 3 different experts, among them expert 0 and expert 16 - 1. `replica_hot`: every entry of hot_experts is named by some index. `cache_lengths`: the 32 sequences of each device include one with 32 live entries. `routes`: each row names 8 different experts; every expert is named by some row.
All inputs are finite; a program needn't handle non-finite values.
Results may differ from a plain program's by a relative error of at most 0.001.
The roundings to bfloat16 on the way count: a program that leaves them out, or rounds other values in their place, can miss the bound.
Values may be sent and summed in bfloat16 or wider, within the bound.
No kernel may reach another device: no remote copies, remote signals or barrier semaphores. Data moves between devices by JAX's collectives and lax.ppermute only.
A program may use at most 64 MiB of HBM per device.

v0:
```python
import math
import jax
import jax.numpy as jnp
from jax import lax
from jax.sharding import PartitionSpec as P

HEADS = 32
KV_HEADS = 4
HEAD = 128
TOP = 8
CAP = 3
SLOTS = 2
norm_epsilon = 1e-06


def spread(shard, axis, root):
    mine = lax.axis_index(axis) == root
    return lax.psum(jnp.where(mine, shard, jnp.zeros_like(shard)), axis)


def scaled_norm(hidden_rows, norm_gain):
    values = hidden_rows.astype(jnp.float32)
    mean_square = jnp.mean(values * values, axis=-1, keepdims=True)
    return (values * lax.rsqrt(mean_square + norm_epsilon) * norm_gain.astype(jnp.float32)).astype(
        jnp.bfloat16
    )


def table_lookup(onehot_rows, table):
    return jnp.dot(onehot_rows, table, preferred_element_type=jnp.int32)


def attend(query_rows, key_cache, value_cache, new_keys, new_values, cache_lengths, step_index):
    rows_here = query_rows.shape[0]
    cache_len = key_cache.shape[1]
    steps_all = new_keys.shape[0]
    grouped = query_rows.reshape(rows_here, KV_HEADS, HEADS // KV_HEADS, HEAD)
    keys_cached = key_cache.reshape(rows_here, cache_len, KV_HEADS, HEAD)
    values_cached = value_cache.reshape(rows_here, cache_len, KV_HEADS, HEAD)
    keys_fresh = new_keys.reshape(steps_all, rows_here, KV_HEADS, HEAD)
    values_fresh = new_values.reshape(steps_all, rows_here, KV_HEADS, HEAD)
    score_scale = 1.0 / math.sqrt(HEAD)
    cache_scores = (
        jnp.einsum("rkgh,rckh->rkgc", grouped, keys_cached, preferred_element_type=jnp.float32)
        * score_scale
    )
    fresh_scores = (
        jnp.einsum("rkgh,srkh->rkgs", grouped, keys_fresh, preferred_element_type=jnp.float32)
        * score_scale
    )
    cache_mask = (jnp.arange(cache_len, dtype=jnp.int32)[None, :] < cache_lengths[:, None])[
        :, None, None, :
    ]
    fresh_mask = (jnp.arange(steps_all, dtype=jnp.int32) <= step_index)[None, None, None, :]
    row_max = jnp.maximum(
        jnp.max(jnp.where(cache_mask, cache_scores, -1e30), axis=-1),
        jnp.max(jnp.where(fresh_mask, fresh_scores, -1e30), axis=-1),
    )
    cache_exp = jnp.where(cache_mask, jnp.exp(cache_scores - row_max[..., None]), 0.0)
    fresh_exp = jnp.where(fresh_mask, jnp.exp(fresh_scores - row_max[..., None]), 0.0)
    row_total = jnp.sum(cache_exp, axis=-1) + jnp.sum(fresh_exp, axis=-1)
    cache_probs = (cache_exp / row_total[..., None]).astype(jnp.bfloat16)
    fresh_probs = (fresh_exp / row_total[..., None]).astype(jnp.bfloat16)
    summed = jnp.einsum(
        "rkgc,rckh->rkgh", cache_probs, values_cached, preferred_element_type=jnp.float32
    )
    summed = summed + jnp.einsum(
        "rkgs,srkh->rkgh", fresh_probs, values_fresh, preferred_element_type=jnp.float32
    )
    return summed.astype(jnp.bfloat16).reshape(rows_here, HEADS * HEAD)


def body(
    hidden,
    norm_gain,
    gate_weights,
    routes,
    replica_pick,
    trainer_experts,
    hot_experts,
    replica_hot,
    w_gate,
    w_up,
    w_down,
    queries,
    key_cache,
    value_cache,
    new_keys,
    new_values,
    cache_lengths,
):
    ep_count = lax.axis_size("ep")
    my_device = lax.axis_index("ep")
    device_ids = jnp.arange(ep_count, dtype=jnp.int32)
    expert_count = trainer_experts.shape[0]
    expert_ids = jnp.arange(expert_count, dtype=jnp.int32)
    hot_count = hot_experts.shape[0]
    hot_ids = jnp.arange(hot_count, dtype=jnp.int32)
    home_device = jnp.sum(
        jnp.where(trainer_experts[None, :] == expert_ids[:, None], device_ids[None, :], 0), axis=1
    )
    hosted = jnp.sum(
        jnp.where(replica_hot[:, None] == hot_ids[None, :], hot_experts[None, :], 0), axis=1
    )
    is_replica = (hosted[None, :] == expert_ids[:, None]).astype(jnp.int32)
    replica_order = jnp.cumsum(is_replica, axis=1) * is_replica
    copies = 1 + jnp.sum(is_replica, axis=1)
    my_hot = jnp.sum(jnp.where(device_ids == my_device, replica_hot, 0))
    own_pair = jnp.concatenate([w_gate, w_up], axis=0)
    own_full_pair, own_full_down = (
        lax.all_gather(own_pair, "dp", axis=1, tiled=True),
        lax.all_gather(w_down, "dp", axis=2, tiled=True),
    )
    replica_pair = jnp.zeros_like(own_pair)
    replica_down = jnp.zeros_like(w_down)
    for hot_index in range(hot_count):
        hot_expert = jnp.sum(jnp.where(hot_ids == hot_index, hot_experts, 0))
        root_device = jnp.sum(jnp.where(expert_ids == hot_expert, home_device, 0))
        sent_pair, sent_down = (
            spread(own_pair, "ep", root_device),
            spread(w_down, "ep", root_device),
        )
        wanted = my_hot == hot_index
        replica_pair = jnp.where(wanted, sent_pair, replica_pair)
        replica_down = jnp.where(wanted, sent_down, replica_down)
    replica_full_pair, replica_full_down = (
        lax.all_gather(replica_pair, "dp", axis=1, tiled=True),
        lax.all_gather(replica_down, "dp", axis=2, tiled=True),
    )
    slot_pair = jnp.stack([own_full_pair, replica_full_pair])
    slot_down = jnp.concatenate([own_full_down, replica_full_down], axis=0)
    tokens_here = hidden.shape[1]
    width = hidden.shape[2]
    entries = tokens_here * TOP
    slot_total = ep_count * SLOTS
    buffer_rows = slot_total * CAP
    entry_ids = jnp.arange(entries, dtype=jnp.int32)
    token_map = (
        (entry_ids // TOP)[:, None] == jnp.arange(tokens_here, dtype=jnp.int32)[None, :]
    ).astype(jnp.float32)
    contract_first = (((0,), (0,)), ((), ()))
    mixed_steps = []
    context_steps = []
    for step_index in range(hidden.shape[0]):
        context_steps.append(
            attend(
                queries[step_index],
                key_cache,
                value_cache,
                new_keys,
                new_values,
                cache_lengths,
                step_index,
            )
        )
        normed = scaled_norm(hidden[step_index], norm_gain)
        weights_top = gate_weights[step_index]
        gates = (weights_top / jnp.sum(weights_top, axis=-1, keepdims=True)).astype(jnp.bfloat16)
        chosen = routes[step_index].reshape(entries)
        replica_picks = replica_pick[step_index].reshape(entries)
        expert_onehot = (chosen[:, None] == expert_ids[None, :]).astype(jnp.int32)
        replica_index = replica_picks % table_lookup(expert_onehot, copies)
        order_rows = table_lookup(expert_onehot, replica_order)
        replica_device = jnp.sum(
            jnp.where(order_rows == replica_index[:, None], device_ids[None, :], 0), axis=1
        )
        target = jnp.where(
            replica_index == 0, table_lookup(expert_onehot, home_device), replica_device
        )
        second_slot = (replica_index > 0).astype(jnp.int32)
        slot_index = target * SLOTS + second_slot
        slot_onehot = (
            slot_index[:, None] == jnp.arange(slot_total, dtype=jnp.int32)[None, :]
        ).astype(jnp.int32)
        slot_rank = jnp.sum(jnp.cumsum(slot_onehot, axis=0) * slot_onehot, axis=1) - 1
        is_kept = slot_rank < CAP
        row_index = second_slot * (ep_count * CAP) + target * CAP + slot_rank
        placed = (
            is_kept[:, None]
            & (row_index[:, None] == jnp.arange(buffer_rows, dtype=jnp.int32)[None, :])
        ).astype(jnp.float32)
        dispatch = lax.dot_general(placed, token_map, contract_first).astype(jnp.bfloat16)
        weighted = placed * gates.reshape(entries).astype(jnp.float32)[:, None]
        combine_map = lax.dot_general(token_map, weighted, contract_first).astype(jnp.bfloat16)
        outgoing = jnp.dot(dispatch, normed, preferred_element_type=jnp.float32).astype(
            jnp.bfloat16
        )
        outgoing = outgoing.reshape(SLOTS, ep_count, CAP, width)
        incoming = lax.all_to_all(outgoing, "ep", split_axis=1, concat_axis=1, tiled=True)
        slot_rows = incoming.reshape(SLOTS, ep_count * CAP, width)
        projected = jnp.einsum(
            "snd,skdf->sknf", slot_rows, slot_pair, preferred_element_type=jnp.float32
        )
        hidden_units = (jax.nn.silu(projected[:, 0]) * projected[:, 1]).astype(jnp.bfloat16)
        expert_out = jnp.einsum(
            "snf,sfd->snd", hidden_units, slot_down, preferred_element_type=jnp.float32
        ).astype(jnp.bfloat16)
        expert_out = expert_out.reshape(SLOTS, ep_count, CAP, width)
        returned = lax.all_to_all(
            expert_out, "ep", split_axis=1, concat_axis=1, tiled=True
        ).reshape(buffer_rows, width)
        mixed_rows = hidden[step_index].astype(jnp.float32) + jnp.dot(
            combine_map, returned, preferred_element_type=jnp.float32
        )
        mixed_steps.append(mixed_rows.astype(jnp.bfloat16))
    return (jnp.stack(mixed_steps), jnp.stack(context_steps))


def solution(mesh):
    return jax.shard_map(
        body,
        mesh=mesh,
        in_specs=(
            P(None, ("ep", "dp"), None),
            P(),
            P(None, ("ep", "dp"), None),
            P(None, ("ep", "dp"), None),
            P(None, ("ep", "dp"), None),
            P(),
            P(),
            P(),
            P("ep", "dp", None),
            P("ep", "dp", None),
            P("ep", None, "dp"),
            P(None, ("ep", "dp"), None),
            P(("ep", "dp"), None, None),
            P(("ep", "dp"), None, None),
            P(None, ("ep", "dp"), None),
            P(None, ("ep", "dp"), None),
            P(("ep", "dp")),
        ),
        out_specs=(P(None, ("ep", "dp"), None), P(None, ("ep", "dp"), None)),
        check_vma=False,
    )
```

profile of v0, /device:TPU:0, one launch (start us, length us, event | category | flops | bytes accessed | tf_op | source)
XLA Modules:
  0.0 346.7 jit_solution(13511546393007678465)
XLA Ops:
  8.1 1.5 fusion.144
  9.5 0.8 select_reduce_fusion.4
  10.3 2.7 fusion.145
  14.9 1.2 constant_dynamic-update-slice_fusion.1
  16.1 1.3 constant_dynamic-update-slice_fusion
  17.4 2.3 broadcast_select_fusion
  20.1 1.5 broadcast_select_fusion.3
  27.1 148.3 %all-reduce.3.cloned.1.call-done = (bf16[1,384,1024]{2,1,0:T(8,128)(2,1)}, bf16[1,384,1024]{2,1,0:T(8,128)(2,1)}, bf16[1,384,1024]{2,1,0:T(8,128)(2,1)}, bf16[2,...) async-done(((bf16[1,384,1024]{2,1,0:T(8,128)(2,1)}, bf16[1,384,1024]{2,1,0:T(8,128)(2,1)}, bf16[1,384,1024]{2,1,0:T(8,128)(2,1)}, ...) | async-done | bytes 7077904 | tf_op jit(solution)/shard_map/psum | solution.py:18
  175.4 2.1 select_select_fusion.1
  180.8 1.2 copy.85
  182.0 5.0 %all-to-all-start = ((bf16[2,16,3,2048]{3,0,2,1:T(2,128)(2,1)}), bf16[2,16,3,2048]{3,0,2,1:T(2,128)(2,1)S(1)}, u32[]{:S(2)}, u32[]{:S(2)}) async-start(bf16[2,16,3,2048]{3,0,2,1:T(2,128)(2,1)} %copy.85), calls=%async_computation | async-start | bytes 786432 | tf_op jit(solution)/shard_map/all_to_all | solution.py:189
  191.4 1.2 copy.94
  192.6 0.7 iota_compare_fusion.23
  193.4 2.9 select_select_fusion
  196.7 0.8 select_reduce_fusion.1
  197.5 1.2 select_reduce_fusion.2
  198.7 0.8 fusion.23
  202.5 2.7 constant_dynamic-update-slice_fusion.3
  205.3 2.8 constant_dynamic-update-slice_fusion.2
  208.1 6.0 %all-to-all-start.2 = ((bf16[2,16,3,2048]{3,0,2,1:T(2,128)(2,1)}), bf16[2,16,3,2048]{3,0,2,1:T(2,128)(2,1)S(1)}, u32[]{:S(2)}, u32[]{:S(2)}) async-start(bf16[2,16,3,2048]{3,0,2,1:T(2,128)(2,1)} %copy.94), calls=%async_computation.2 | async-start | bytes 786432 | tf_op jit(solution)/shard_map/all_to_all | solution.py:189
  214.1 37.0 %all-gather.5.cloned.1.call-done = bf16[2,2048,384]{2,1,0:T(8,128)(2,1)} async-done(((bf16[2,1024,384]{2,1,0:T(8,128)(2,1)}), bf16[2,2048,384]{2,1,0:T(8,128)(2,1)}) %all-gather.5.cloned.1.call-update) | async-done | bytes 3145744 | tf_op jit(solution)/shard_map/all_gather | solution.py:111
  251.1 46.4 %all-gather.7.cloned.1.call-done = bf16[2,2048,384]{2,1,0:T(8,128)(2,1)} async-done(((bf16[2,1024,384]{2,1,0:T(8,128)(2,1)}), bf16[2,2048,384]{2,1,0:T(8,128)(2,1)}) %all-gather.7.cloned.1.call-update) | async-done | bytes 3145744 | tf_op jit(solution)/shard_map/all_gather | solution.py:127
  297.5 3.6 %convolution_bitcast_fusion = f32[2,2,48,384]{3,2,1,0:T(8,128)S(1)} fusion(bf16[2,48,2048,1]{2,0,1,3:T(2,128)(2,1)S(1)} %bitcast.161, bf16[1,2,2048,384]{3,2,1,0:T(8,128)(2,1)} %bitcast.175, bf16[1,2,2048,384]{3,2,1,0:T(8,128)(2,1)} %bitcast.173), kind=kOutput, calls=%fused_computation.24 | convolution fusion | flops 314572800 | bytes 6979584 | tf_op jit(solution)/shard_map/snd,skdf->sknf/dot_general | solution.py:191
  301.9 1.2 copy.88
  303.0 5.6 %all-to-all-start.1 = ((bf16[2,16,3,2048]{3,0,2,1:T(2,128)(2,1)}), bf16[2,16,3,2048]{3,0,2,1:T(2,128)(2,1)S(1)}, u32[]{:S(2)}, u32[]{:S(2)}) async-start(bf16[2,16,3,2048]{3,0,2,1:T(2,128)(2,1)} %bitcast.15), calls=%async_computation.1 | async-start | bytes 786432 | tf_op jit(solution)/shard_map/all_to_all | solution.py:199
  308.7 3.6 %fusion.8 = f32[2,2,48,384]{3,2,0,1:T(8,128)S(1)} fusion(bf16[2,48,2048]{2,0,1:T(2,128)(2,1)S(1)} %bitcast.162, bf16[1,2,2048,384]{3,2,1,0:T(8,128)(2,1)} %bitcast.176, bf16[1,2,2048,384]{3,2,1,0:T(8,128)(2,1)} %bitcast.174), kind=kOutput, calls=%fused_computation.23 | convolution fusion | flops 305135616 | bytes 6979584 | tf_op jit(solution)/shard_map/snd,skdf->sknf/dot_general | solution.py:191
  313.1 1.2 copy.97
  314.2 6.6 %all-to-all-done.1 = bf16[2,16,3,2048]{3,0,2,1:T(2,128)(2,1)S(1)} async-done(((bf16[2,16,3,2048]{3,0,2,1:T(2,128)(2,1)}), bf16[2,16,3,2048]{3,0,2,1:T(2,128)(2,1)S(1)}, u32[]{:S(2)}, u32[]{:S(2)}) %all-to-all-start.1) | async-done | bytes 393248 | tf_op jit(solution)/shard_map/all_to_all | solution.py:199
  320.8 3.7 %all-to-all-start.3 = ((bf16[2,16,3,2048]{3,0,2,1:T(2,128)(2,1)}), bf16[2,16,3,2048]{3,0,2,1:T(2,128)(2,1)S(1)}, u32[]{:S(2)}, u32[]{:S(2)}) async-start(bf16[2,16,3,2048]{3,0,2,1:T(2,128)(2,1)} %bitcast.30), calls=%async_computation.3 | async-start | bytes 786432 | tf_op jit(solution)/shard_map/all_to_all | solution.py:199
  325.1 0.8 pad_maximum_fusion.1
  326.6 10.1 %all-to-all-done.3 = bf16[2,16,3,2048]{3,0,2,1:T(2,128)(2,1)S(1)} async-done(((bf16[2,16,3,2048]{3,0,2,1:T(2,128)(2,1)}), bf16[2,16,3,2048]{3,0,2,1:T(2,128)(2,1)S(1)}, u32[]{:S(2)}, u32[]{:S(2)}) %all-to-all-start.3) | async-done | bytes 393248 | tf_op jit(solution)/shard_map/all_to_all | solution.py:199
  338.4 0.7 pad_maximum_fusion.2
  (164 shorter events, 18.9 us)
Async XLA Ops:
  8.0 193.5 %copy-start = (bf16[32,32,512]{2,1,0:T(8,128)(2,1)S(1)}, bf16[32,32,512]{2,1,0:T(8,128)(2,1)}, u32[]{:S(2)}) copy-start(bf16[32,32,512]{2,1,0:T(8,128)(2,1)} %param.30) | copy-start | bytes 3145732
  8.0 167.4 %all-reduce.3.cloned.1.call-start = ((), (), s32[]{:S(2)}) async-start(), calls=%async_computation.8 | async-start | bytes 14155776 | tf_op jit(solution)/shard_map/psum | solution.py:18
  10.3 16.5 %copy-start.23 = (s32[16]{0:T(128)}, s32[16]{0:T(128)S(1)}, u32[]{:S(2)}) copy-start(s32[16]{0:T(128)S(1)} %select_reduce_fusion.4) | copy-start | bytes 196
  21.5 3.6 %copy-start.15 = (s32[2,32,8]{1,2,0:T(8,128)S(1)}, s32[2,32,8]{1,2,0:T(8,128)}, u32[]{:S(2)}) copy-start(s32[2,32,8]{1,2,0:T(8,128)} %param.21) | copy-start | bytes 6148
  21.6 156.8 %copy-start.19 = (bf16[2048]{0:T(1024)(128)(2,1)S(1)}, bf16[2048]{0:T(1024)(128)(2,1)}, u32[]{:S(2)}) copy-start(bf16[2048]{0:T(1024)(128)(2,1)} %param.18) | copy-start | bytes 12292
  21.6 156.9 %copy-start.5 = (bf16[2,32,2048]{2,1,0:T(8,128)(2,1)S(1)}, bf16[2,32,2048]{2,1,0:T(8,128)(2,1)}, u32[]{:S(2)}) copy-start(bf16[2,32,2048]{2,1,0:T(8,128)(2,1)} %param.17) | copy-start | bytes 786436
  21.6 180.9 %all-gather.9.cloned.1.call-start = ((), (), s32[]{:S(2)}) async-start(), calls=%async_computation.6 | async-start | bytes 2359296 | tf_op jit(solution)/shard_map/all_gather | solution.py:112
  22.2 183.1 %all-gather.11.cloned.1.call-start = ((), (), s32[]{:S(2)}) async-start(), calls=%async_computation.7 | async-start | bytes 2359296 | tf_op jit(solution)/shard_map/all_gather | solution.py:128
  23.0 3.6 %copy-start.25 = (s32[16]{0:T(128)}, s32[16]{0:T(128)S(1)}, u32[]{:S(2)}) copy-start(s32[16]{0:T(128)S(1)} %select_reduce_fusion.5) | copy-start | bytes 196
  26.0 153.2 %copy-start.17 = (s32[16,16]{1,0:T(8,128)}, s32[16,16]{1,0:T(8,128)S(1)}, u32[]{:S(2)}) copy-start(s32[16,16]{1,0:T(8,128)S(1)} %reduce_window_sum.36) | copy-start | bytes 3076
  26.2 153.1 %copy-start.29 = (s32[16]{0:T(128)}, s32[16]{0:T(128)S(1)}, u32[]{:S(2)}) copy-start(s32[16]{0:T(128)S(1)} %fusion.138) | copy-start | bytes 196
  177.5 10.1 %copy-start.7 = (bf16[2,32,4096]{2,1,0:T(8,128)(2,1)S(1)}, bf16[2,32,4096]{2,1,0:T(8,128)(2,1)}, u32[]{:S(2)}) copy-start(bf16[2,32,4096]{2,1,0:T(8,128)(2,1)} %param.28) | copy-start | bytes 1572868
  179.8 7.9 %copy-start.8 = (bf16[2,32,512]{2,1,0:T(8,128)(2,1)S(1)}, bf16[2,32,512]{2,1,0:T(8,128)(2,1)}, u32[]{:S(2)}) copy-start(bf16[2,32,512]{2,1,0:T(8,128)(2,1)} %param.31) | copy-start | bytes 196612
  180.4 7.4 %copy-start.9 = (bf16[2,32,512]{2,1,0:T(8,128)(2,1)S(1)}, bf16[2,32,512]{2,1,0:T(8,128)(2,1)}, u32[]{:S(2)}) copy-start(bf16[2,32,512]{2,1,0:T(8,128)(2,1)} %param.32) | copy-start | bytes 196612
  180.7 7.2 %copy-start.16 = (f32[2,32,8]{1,2,0:T(8,128)S(1)}, f32[2,32,8]{1,2,0:T(8,128)}, u32[]{:S(2)}) copy-start(f32[2,32,8]{1,2,0:T(8,128)} %param.19) | copy-start | bytes 6148
  180.7 7.7 %copy-start.11 = (s32[1,32,8]{1,2,0:T(8,128)S(1)}, s32[1,32,8]{1,2,0:T(8,128)}, u32[]{:S(2)}) copy-start(s32[1,32,8]{1,2,0:T(8,128)} %get-tuple-element.32) | copy-start | bytes 3076
  180.7 7.9 %copy-start.30 = (s32[16]{0:T(128)S(1)}, s32[16]{0:T(128)}, u32[]{:S(2)}) copy-start(s32[16]{0:T(128)} %copy-done.29) | copy-start | bytes 196
  180.7 8.3 %copy-start.18 = (s32[16,16]{1,0:T(8,128)S(1)}, s32[16,16]{1,0:T(8,128)}, u32[]{:S(2)}) copy-start(s32[16,16]{1,0:T(8,128)} %copy-done.17) | copy-start | bytes 3076
  180.7 8.3 %copy-start.26 = (s32[16]{0:T(128)S(1)}, s32[16]{0:T(128)}, u32[]{:S(2)}) copy-start(s32[16]{0:T(128)} %copy-done.25) | copy-start | bytes 196
  180.7 8.6 %copy-start.24 = (s32[16]{0:T(128)S(1)}, s32[16]{0:T(128)}, u32[]{:S(2)}) copy-start(s32[16]{0:T(128)} %copy-done.23) | copy-start | bytes 196
  182.0 8.6 %copy-start.22 = (f32[32]{0:T(128)S(1)}, f32[32]{0:T(128)}, u32[]{:S(2)}) copy-start(f32[32]{0:T(128)} %get-tuple-element.41) | copy-start | bytes 388
  182.0 26.1 %all-to-all-start = ((bf16[2,16,3,2048]{3,0,2,1:T(2,128)(2,1)}), bf16[2,16,3,2048]{3,0,2,1:T(2,128)(2,1)S(1)}, u32[]{:S(2)}, u32[]{:S(2)}) async-start(bf16[2,16,3,2048]{3,0,2,1:T(2,128)(2,1)} %copy.85), calls=%async_computation | async-start | bytes 786432 | tf_op jit(solution)/shard_map/all_to_all | solution.py:189
  187.0 64.1 %all-gather.5.cloned.1.call-start = ((), (), s32[]{:S(2)}) async-start(), calls=%async_computation.4 | async-start | bytes 4718592 | tf_op jit(solution)/shard_map/all_gather | solution.py:111
  187.6 109.9 %all-gather.7.cloned.1.call-start = ((), (), s32[]{:S(2)}) async-start(), calls=%async_computation.5 | async-start | bytes 4718592 | tf_op jit(solution)/shard_map/all_gather | solution.py:127
  187.8 8.5 %copy-start.10 = (bf16[2,32,4,128]{3,2,1,0:T(4,128)(2,1)}, bf16[2,32,4,128]{3,2,1,0:T(4,128)(2,1)S(1)}, u32[]{:S(2)}) copy-start(bf16[2,32,4,128]{3,2,1,0:T(4,128)(2,1)S(1)} %reshape.214) | copy-start | bytes 196612
  208.1 95.0 %all-to-all-start.2 = ((bf16[2,16,3,2048]{3,0,2,1:T(2,128)(2,1)}), bf16[2,16,3,2048]{3,0,2,1:T(2,128)(2,1)S(1)}, u32[]{:S(2)}, u32[]{:S(2)}) async-start(bf16[2,16,3,2048]{3,0,2,1:T(2,128)(2,1)} %copy.94), calls=%async_computation.2 | async-start | bytes 786432 | tf_op jit(solution)/shard_map/all_to_all | solution.py:189
  297.5 3.8 %copy-start.1 = (bf16[2,384,2048]{2,1,0:T(8,128)(2,1)S(1)}, bf16[2,384,2048]{2,1,0:T(8,128)(2,1)}, u32[]{:S(2)}) copy-start(bf16[2,384,2048]{2,1,0:T(8,128)(2,1)} %constant_dynamic-update-slice_fusion.2) | copy-start | bytes 9437188
  303.0 17.8 %all-to-all-start.1 = ((bf16[2,16,3,2048]{3,0,2,1:T(2,128)(2,1)}), bf16[2,16,3,2048]{3,0,2,1:T(2,128)(2,1)S(1)}, u32[]{:S(2)}, u32[]{:S(2)}) async-start(bf16[2,16,3,2048]{3,0,2,1:T(2,128)(2,1)} %bitcast.15), calls=%async_computation.1 | async-start | bytes 786432 | tf_op jit(solution)/shard_map/all_to_all | solution.py:199
  308.7 3.8 %copy-start.2 = (bf16[2,384,2048]{2,1,0:T(8,128)(2,1)S(1)}, bf16[2,384,2048]{2,1,0:T(8,128)(2,1)}, u32[]{:S(2)}) copy-start(bf16[2,384,2048]{2,1,0:T(8,128)(2,1)} %constant_dynamic-update-slice_fusion.2) | copy-start | bytes 9437188
  320.8 16.4 %copy-start.13 = (s32[256]{0:T(256)S(1)}, s32[256]{0:T(256)}, u32[]{:S(2)}) copy-start(s32[256]{0:T(256)} %copy-done.12) | copy-start | bytes 3076
  320.8 16.5 %copy-start.21 = (pred[256]{0:T(512)(128)(4,1)S(1)}, pred[256]{0:T(512)(128)(4,1)}, u32[]{:S(2)}) copy-start(pred[256]{0:T(512)(128)(4,1)} %copy-done.20) | copy-start | bytes 772
  320.8 15.8 %all-to-all-start.3 = ((bf16[2,16,3,2048]{3,0,2,1:T(2,128)(2,1)}), bf16[2,16,3,2048]{3,0,2,1:T(2,128)(2,1)S(1)}, u32[]{:S(2)}, u32[]{:S(2)}) async-start(bf16[2,16,3,2048]{3,0,2,1:T(2,128)(2,1)} %bitcast.30), calls=%async_computation.3 | async-start | bytes 786432 | tf_op jit(solution)/shard_map/all_to_all | solution.py:199
  (8 other events, 15.2 us)
Sparse Core Ops, SparseCore 0:
  21.7 153.6 all-reduce.2
Sparse Core Ops, SparseCore 1:
  23.6 29.7 all-gather.8
  177.7 27.2 all-gather.10
  206.3 44.7 all-gather.4
  252.7 44.7 all-gather.6
where the time goes:
time: 348 us; the launch traced here: 347 us
  waiting for transfers between devices  249 us (72%)
  other arithmetic  20.8 us (6%)
  starting transfers between devices  20.5 us (6%)
  between operations  20.2 us (6%)
  local copies, waits for them, and re-layouts  18.5 us (5%)
  matrix products  17.3 us (5%)
    psum x1, waiting for transfers between devices, spread(): return lax.psum(jnp.where(mine, shard, jnp.zeros_like(shard)), axis)  148 us
    all_gather x1, waiting for transfers between devices, body(): lax.all_gather(replica_pair, 'dp', axis=1, tiled=True)  46.4 us
    all_gather x1, waiting for transfers between devices, body(): lax.all_gather(own_pair, 'dp', axis=1, tiled=True)  37 us
    all_to_all x2, waiting for transfers between devices, body(): lax.all_to_all(expert_out, 'ep', split_axis=1, concat_axis=1, tiled=True)  16.7 us
    all_to_all x2, starting transfers between devices, body(): lax.all_to_all(outgoing, 'ep', split_axis=1, concat_axis=1, tiled=True)  11 us
    all_to_all x2, starting transfers between devices, body(): lax.all_to_all(expert_out, 'ep', split_axis=1, concat_axis=1, tiled=True)  9.3 us
    dot_general x2, matrix products, body(): jnp.einsum('snd,skdf->sknf', slot_rows, slot_pair, preferred_element_type...  7.23 us
  transfers between devices with their start and end apart: 9, of which 5 were waited for; matrix products, arithmetic and copies ran while one was open for 12% of the time, Pallas kernels for 0%

commit v1 on v0

--- a/solution.py
+++ b/solution.py
@@ -11,6 +11,18 @@
 CAP = 3
 SLOTS = 2
 norm_epsilon = 1e-06
+
+
+def gather_by_bits(array, axis, dim):
+    ways, here = (lax.axis_size(axis), lax.axis_index(axis))
+    grown, reach = (array, 1)
+    while reach < ways:
+        theirs = lax.ppermute(grown, axis, [(d, d ^ reach) for d in range(ways)])
+        mine_first = jnp.concatenate([grown, theirs], axis=dim)
+        theirs_first = jnp.concatenate([theirs, grown], axis=dim)
+        grown = jnp.where(here & reach == 0, mine_first, theirs_first)
+        reach = 2 * reach
+    return grown
 
 
 def spread(shard, axis, root):
@@ -108,7 +120,7 @@
     my_hot = jnp.sum(jnp.where(device_ids == my_device, replica_hot, 0))
     own_pair = jnp.concatenate([w_gate, w_up], axis=0)
     own_full_pair, own_full_down = (
-        lax.all_gather(own_pair, "dp", axis=1, tiled=True),
+        gather_by_bits(own_pair, "dp", 1),
         lax.all_gather(w_down, "dp", axis=2, tiled=True),
     )
     replica_pair = jnp.zeros_like(own_pair)

time: 348 us -> 309 us (0.89)
  waiting for transfers between devices: 249 us -> 187 us
  matrix products: 17.3 us -> 25.1 us
  other arithmetic: 20.8 us -> 27.6 us
  local copies, waits for them, and re-layouts: 18.5 us -> 24.1 us
    all_gather x1 -> x0, waiting for transfers between devices: 37 us -> none  [body(): lax.all_gather(own_pair, 'dp', axis=1, tiled=True)]
    psum x1, waiting for transfers between devices: 148 us -> 133 us  [spread(): return lax.psum(jnp.where(mine, shard, jnp.zeros_like(shard)), axis)]
    all_gather x1, waiting for transfers between devices: 46.4 us -> 36.4 us  [body(): lax.all_gather(replica_pair, 'dp', axis=1, tiled=True)]
    dot_general x2, matrix products: 1.59 us -> 5.58 us  [attend(): jnp.einsum('rkgh,rckh->rkgc', grouped, keys_cached, preferred_element_typ...]
    select_n x0 -> x1, other arithmetic: none -> 3.9 us  [gather_by_bits(): grown = jnp.where(here & reach == 0, mine_first, theirs_first)]
    unnamed x67 -> x111, local copies, waits for them, and re-layouts: 5.35 us -> 7.85 us
  transfers between devices with their start and end apart: 9 -> 9, of which waited for: 5 -> 4; matrix products, arithmetic and copies ran while one was open for 12% -> 20% of each run, Pallas kernels for 0% -> 0%
where the time goes in v1:
time: 309 us; the launch traced here: 308 us
  waiting for transfers between devices  187 us (61%)
  other arithmetic  27.6 us (9%)
  matrix products  25.1 us (8%)
  local copies, waits for them, and re-layouts  24.1 us (8%)
  starting transfers between devices  23.5 us (8%)
  between operations  20.2 us (7%)
    psum x1, waiting for transfers between devices, spread(): return lax.psum(jnp.where(mine, shard, jnp.zeros_like(shard)), axis)  133 us
    all_gather x1, waiting for transfers between devices, body(): lax.all_gather(replica_pair, 'dp', axis=1, tiled=True)  36.4 us
    all_to_all x2, waiting for transfers between devices, body(): lax.all_to_all(expert_out, 'ep', split_axis=1, concat_axis=1, tiled=True)  16.6 us
    all_to_all x2, starting transfers between devices, body(): lax.all_to_all(outgoing, 'ep', split_axis=1, concat_axis=1, tiled=True)  10.9 us
    all_to_all x2, starting transfers between devices, body(): lax.all_to_all(expert_out, 'ep', split_axis=1, concat_axis=1, tiled=True)  9.3 us
    unnamed x111, local copies, waits for them, and re-layouts  7.85 us
    dot_general x2, matrix products, body(): jnp.einsum('snd,skdf->sknf', slot_rows, slot_pair, preferred_element_type...  7.42 us
  transfers between devices with their start and end apart: 9, of which 4 were waited for; matrix products, arithmetic and copies ran while one was open for 20% of the time, Pallas kernels for 0%

profile of v1, /device:TPU:0, one launch (start us, length us, event | category | flops | bytes accessed | tf_op | source)
XLA Modules:
  0.0 307.6 jit_solution(3580631024851828832)
XLA Ops:
  8.1 1.5 fusion.144
  10.3 2.7 fusion.145
  16.1 1.3 constant_dynamic-update-slice_fusion
  17.4 2.3 broadcast_select_fusion
  19.7 1.5 broadcast_select_fusion.3
  21.2 3.0 collective-permute-start
  28.0 1.3 convolution_convert_fusion.3
  29.4 1.5 reshape.259
  32.1 6.0 %all-to-all-start = ((bf16[2,16,3,2048]{3,0,2,1:T(2,128)(2,1)}), bf16[2,16,3,2048]{3,0,2,1:T(2,128)(2,1)}, u32[]{:S(2)}, u32[]{:S(2)}) async-start(bf16[2,16,3,2048]{3,0,2,1:T(2,128)(2,1)} %copy.85), calls=%async_computation | async-start | bytes 786432 | tf_op jit(solution)/shard_map/all_to_all | solution.py:201
  40.6 1.3 fusion.139
  47.9 1.3 select_reduce_fusion.3
  49.2 133.4 %all-reduce.3.cloned.1.call-done = (bf16[1,384,1024]{2,1,0:T(8,128)(2,1)}, bf16[1,384,1024]{2,1,0:T(8,128)(2,1)}, bf16[1,384,1024]{2,1,0:T(8,128)(2,1)}, bf16[2,...) async-done(((bf16[1,384,1024]{2,1,0:T(8,128)(2,1)}, bf16[1,384,1024]{2,1,0:T(8,128)(2,1)}, bf16[1,384,1024]{2,1,0:T(8,128)(2,1)}, ...) | async-done | bytes 7077904 | tf_op jit(solution)/shard_map/psum | solution.py:30
  182.6 2.1 select_select_fusion.1
  185.1 2.1 select_reduce_fusion.1
  187.3 1.4 select_reduce_fusion.2
  188.8 3.5 %fusion.23 = (f32[32,4,8]{2,1,0:T(4,128)}, f32[32,4,8]{2,1,0:T(4,128)S(1)}, f32[32,4,8,32]{3,2,1,0:T(8,128)}) fusion(f32[32,4,8,32]{3,2,1,0:T(8,128)S(1)} %get-tuple-element.35, f32[32,4,8]{2,1,0:T(4,128)S(1)} %max.14, pred[32,32]{1,0:T(8,128)(4,1)S(1)} %iota_compare_fusion.23, bf16[32,4,8,128]{3,2,1,0:T(8,128)(2,1)} %bitcast.165, ...), kind=kOutput, calls=%fused_computation.57 | convolution fusion | flops 8583168 | bytes 1586176 | tf_op jit(solution)/shard_map/rkgh,rckh->rkgc/dot_general | solution.py:56
  192.5 1.4 select_select_fusion
  195.1 1.4 convolution_convert_fusion.1
  198.6 1.4 reshape.264
  202.3 1.4 fusion.24
  204.6 1.3 fusion.78
  207.5 2.7 constant_dynamic-update-slice_fusion.3
  210.3 3.9 %maximum_select_fusion = bf16[1,2,2048,384]{3,2,1,0:T(8,128)(2,1)} fusion(bf16[1,2,1024,384]{3,2,1,0:T(8,128)(2,1)} %bitcast.8, bf16[1,2,1024,384]{3,2,1,0:T(8,128)(2,1)S(1)} %bitcast.160, pred[]{:T(512)S(6)} %eq.293), kind=kLoop, calls=%fused_computation.3 | loop fusion | flops 14155776 | bytes 6291457 | tf_op jit(solution)/shard_map/jit(_where)/select_n | solution.py:23
  214.2 2.8 constant_dynamic-update-slice_fusion.2
  217.0 4.9 %all-to-all-start.2 = ((bf16[2,16,3,2048]{3,0,2,1:T(2,128)(2,1)}), bf16[2,16,3,2048]{3,0,2,1:T(2,128)(2,1)S(1)}, u32[]{:S(2)}, u32[]{:S(2)}) async-start(bf16[2,16,3,2048]{3,0,2,1:T(2,128)(2,1)} %copy.94), calls=%async_computation.2 | async-start | bytes 786432 | tf_op jit(solution)/shard_map/all_to_all | solution.py:201
  221.9 36.4 %all-gather.4.cloned.1.call-done = bf16[2,2048,384]{2,1,0:T(8,128)(2,1)} async-done(((bf16[2,1024,384]{2,1,0:T(8,128)(2,1)}), bf16[2,2048,384]{2,1,0:T(8,128)(2,1)}) %all-gather.4.cloned.1.call-update) | async-done | bytes 3145744 | tf_op jit(solution)/shard_map/all_gather | solution.py:139
  258.3 3.8 %convolution_bitcast_fusion = f32[2,2,48,384]{3,2,1,0:T(8,128)S(1)} fusion(bf16[2,48,2048,1]{2,0,1,3:T(2,128)(2,1)} %bitcast.12, bf16[1,2,2048,384]{3,2,1,0:T(8,128)(2,1)} %bitcast.174, bf16[1,2,2048,384]{3,2,1,0:T(8,128)(2,1)} %maximum_select_fusion), kind=kOutput, calls=%fused_computation.25 | convolution fusion | flops 314572800 | bytes 6979584 | tf_op jit(solution)/shard_map/snd,skdf->sknf/dot_general | solution.py:203
  264.0 5.6 %all-to-all-start.1 = ((bf16[2,16,3,2048]{3,0,2,1:T(2,128)(2,1)}), bf16[2,16,3,2048]{3,0,2,1:T(2,128)(2,1)S(1)}, u32[]{:S(2)}, u32[]{:S(2)}) async-start(bf16[2,16,3,2048]{3,0,2,1:T(2,128)(2,1)} %bitcast.16), calls=%async_computation.1 | async-start | bytes 786432 | tf_op jit(solution)/shard_map/all_to_all | solution.py:211
  269.6 3.6 %fusion.8 = f32[2,2,48,384]{3,2,0,1:T(8,128)S(1)} fusion(bf16[2,48,2048]{2,0,1:T(2,128)(2,1)S(1)} %bitcast.163, bf16[1,2,2048,384]{3,2,1,0:T(8,128)(2,1)} %bitcast.175, bf16[1,2,2048,384]{3,2,1,0:T(8,128)(2,1)} %maximum_select_fusion), kind=kOutput, calls=%fused_computation.24 | convolution fusion | flops 305135616 | bytes 6979584 | tf_op jit(solution)/shard_map/snd,skdf->sknf/dot_general | solution.py:203
  275.2 6.6 %all-to-all-done.1 = bf16[2,16,3,2048]{3,0,2,1:T(2,128)(2,1)S(1)} async-done(((bf16[2,16,3,2048]{3,0,2,1:T(2,128)(2,1)}), bf16[2,16,3,2048]{3,0,2,1:T(2,128)(2,1)S(1)}, u32[]{:S(2)}, u32[]{:S(2)}) %all-to-all-start.1) | async-done | bytes 393248 | tf_op jit(solution)/shard_map/all_to_all | solution.py:211
  281.8 3.7 %all-to-all-start.3 = ((bf16[2,16,3,2048]{3,0,2,1:T(2,128)(2,1)}), bf16[2,16,3,2048]{3,0,2,1:T(2,128)(2,1)S(1)}, u32[]{:S(2)}, u32[]{:S(2)}) async-start(bf16[2,16,3,2048]{3,0,2,1:T(2,128)(2,1)} %bitcast.31), calls=%async_computation.3 | async-start | bytes 786432 | tf_op jit(solution)/shard_map/all_to_all | solution.py:211
  287.6 10.0 %all-to-all-done.3 = bf16[2,16,3,2048]{3,0,2,1:T(2,128)(2,1)S(1)} async-done(((bf16[2,16,3,2048]{3,0,2,1:T(2,128)(2,1)}), bf16[2,16,3,2048]{3,0,2,1:T(2,128)(2,1)S(1)}, u32[]{:S(2)}, u32[]{:S(2)}) %all-to-all-start.3) | async-done | bytes 393248 | tf_op jit(solution)/shard_map/all_to_all | solution.py:211
  (209 shorter events, 30.0 us)
Async XLA Ops:
  8.0 198.4 %copy-start = (bf16[32,32,512]{2,1,0:T(8,128)(2,1)S(1)}, bf16[32,32,512]{2,1,0:T(8,128)(2,1)}, u32[]{:S(2)}) copy-start(bf16[32,32,512]{2,1,0:T(8,128)(2,1)} %param.30) | copy-start | bytes 3145732
  8.0 174.6 %all-reduce.3.cloned.1.call-start = ((), (), s32[]{:S(2)}) async-start(), calls=%async_computation.7 | async-start | bytes 14155776 | tf_op jit(solution)/shard_map/psum | solution.py:30
  21.2 189.0 %collective-permute-start = (bf16[2,1024,384]{2,1,0:T(8,128)(2,1)S(1)}, bf16[2,1024,384]{2,1,0:T(8,128)(2,1)}, u32[]{:S(2)}, u32[]{:S(2)}) collective-permute-start(bf16[2,1024,384]{2,1,0:T(8,128)(2,1)S(1)} %constant_dynamic-update-slice_fusion), channel_id=1, source_target_pairs={{0,1},{1,0},{2,3},{3,2},{4,5},{5,4},{6,7},{7,6},{8,9},{9,8},{10,11... | collective-permute-start | bytes 4718600 | tf_op jit(solution)/shard_map/ppermute | solution.py:20
  25.5 17.1 %copy-start.15 = (bf16[2,32,512]{2,1,0:T(8,128)(2,1)S(1)}, bf16[2,32,512]{2,1,0:T(8,128)(2,1)}, u32[]{:S(2)}) copy-start(bf16[2,32,512]{2,1,0:T(8,128)(2,1)} %param.31) | copy-start | bytes 196612
  27.4 16.7 %copy-start.37 = (pred[256]{0:T(512)(128)(4,1)}, pred[256]{0:T(512)(128)(4,1)S(1)}, u32[]{:S(2)}) copy-start(pred[256]{0:T(512)(128)(4,1)S(1)} %add_compare_fusion.1) | copy-start | bytes 772
  28.0 16.1 %copy-start.19 = (s32[256]{0:T(256)}, s32[256]{0:T(256)S(1)}, u32[]{:S(2)}) copy-start(s32[256]{0:T(256)S(1)} %add_add_fusion.1) | copy-start | bytes 3076
  28.0 12.0 %copy-start.52 = (s32[16]{0:T(128)S(1)}, s32[16]{0:T(128)}, u32[]{:S(2)}) copy-start(s32[16]{0:T(128)} %copy-done.51) | copy-start | bytes 196
  28.0 17.9 %copy-start.44 = (s32[16]{0:T(128)S(1)}, s32[16]{0:T(128)}, u32[]{:S(2)}) copy-start(s32[16]{0:T(128)} %copy-done.43) | copy-start | bytes 196
  32.1 184.9 %all-to-all-start = ((bf16[2,16,3,2048]{3,0,2,1:T(2,128)(2,1)}), bf16[2,16,3,2048]{3,0,2,1:T(2,128)(2,1)}, u32[]{:S(2)}, u32[]{:S(2)}) async-start(bf16[2,16,3,2048]{3,0,2,1:T(2,128)(2,1)} %copy.85), calls=%async_computation | async-start | bytes 786432 | tf_op jit(solution)/shard_map/all_to_all | solution.py:201
  38.1 169.4 %all-gather.6.cloned.1.call-start = ((), (), s32[]{:S(2)}) async-start(), calls=%async_computation.5 | async-start | bytes 2359296 | tf_op jit(solution)/shard_map/all_gather | solution.py:124
  38.7 175.5 %all-gather.8.cloned.1.call-start = ((), (), s32[]{:S(2)}) async-start(), calls=%async_computation.6 | async-start | bytes 2359296 | tf_op jit(solution)/shard_map/all_gather | solution.py:140
  40.6 144.2 %copy-start.23 = (s32[256]{0:T(256)}, s32[256]{0:T(256)S(1)}, u32[]{:S(2)}) copy-start(s32[256]{0:T(256)S(1)} %and_select_fusion) | copy-start | bytes 3076
  41.9 143.1 %copy-start.42 = (s32[32]{0:T(128)S(1)}, s32[32]{0:T(128)}, u32[]{:S(2)}) copy-start(s32[32]{0:T(128)} %param.33) | copy-start | bytes 388
  42.6 142.5 %copy-start.8 = (bf16[4,8,32,128]{3,2,1,0:T(8,128)(2,1)S(1)}, bf16[4,8,32,128]{3,2,1,0:T(8,128)(2,1)}, u32[]{:S(2)}) copy-start(bf16[4,8,32,128]{3,2,1,0:T(8,128)(2,1)} %copy.117) | copy-start | bytes 786436
  46.5 138.3 %copy-start.25 = (s32[256]{0:T(256)}, s32[256]{0:T(256)S(1)}, u32[]{:S(2)}) copy-start(s32[256]{0:T(256)S(1)} %convert_add_fusion) | copy-start | bytes 3076
  47.8 139.4 %copy-start.30 = (s32[32,3]{0,1:T(4,128)}, s32[32,3]{0,1:T(4,128)S(1)}, u32[]{:S(2)}) copy-start(s32[32,3]{0,1:T(4,128)S(1)} %reduce-window.19) | copy-start | bytes 1156
  47.9 139.4 %copy-start.46 = (pred[2]{0:T(512)(128)(4,1)}, pred[2]{0:T(512)(128)(4,1)S(1)}, u32[]{:S(2)}) copy-start(pred[2]{0:T(512)(128)(4,1)S(1)} %iota_compare_fusion.28) | copy-start | bytes 10
  49.2 147.3 %copy-start.12 = (f32[32,4,8,2]{2,3,1,0:T(2,128)}, f32[32,4,8,2]{2,3,1,0:T(2,128)S(1)}, u32[]{:S(2)}) copy-start(f32[32,4,8,2]{2,3,1,0:T(2,128)S(1)} %get-tuple-element.37) | copy-start | bytes 24580
  184.8 73.5 %all-gather.4.cloned.1.call-start = ((), (), s32[]{:S(2)}) async-start(), calls=%async_computation.4 | async-start | bytes 4718592 | tf_op jit(solution)/shard_map/all_gather | solution.py:139
  185.0 7.4 %copy-start.5 = (bf16[2,1024,384]{2,1,0:T(8,128)(2,1)S(1)}, bf16[2,1024,384]{2,1,0:T(8,128)(2,1)}, u32[]{:S(2)}) copy-start(bf16[2,1024,384]{2,1,0:T(8,128)(2,1)} %get-tuple-element.17) | copy-start | bytes 4718596
  185.0 7.4 %copy-start.6 = (bf16[2,1024,384]{2,1,0:T(8,128)(2,1)S(1)}, bf16[2,1024,384]{2,1,0:T(8,128)(2,1)}, u32[]{:S(2)}) copy-start(bf16[2,1024,384]{2,1,0:T(8,128)(2,1)} %get-tuple-element.18) | copy-start | bytes 4718596
  187.3 9.2 %copy-start.48 = (pred[2]{0:T(512)(128)(4,1)}, pred[2]{0:T(512)(128)(4,1)S(1)}, u32[]{:S(2)}) copy-start(pred[2]{0:T(512)(128)(4,1)S(1)} %iota_compare_fusion.27) | copy-start | bytes 10
  188.8 7.7 %copy-start.13 = (f32[32,4,8,2]{2,3,1,0:T(2,128)}, f32[32,4,8,2]{2,3,1,0:T(2,128)S(1)}, u32[]{:S(2)}) copy-start(f32[32,4,8,2]{2,3,1,0:T(2,128)S(1)} %get-tuple-element.40) | copy-start | bytes 24580
  217.0 47.0 %all-to-all-start.2 = ((bf16[2,16,3,2048]{3,0,2,1:T(2,128)(2,1)}), bf16[2,16,3,2048]{3,0,2,1:T(2,128)(2,1)S(1)}, u32[]{:S(2)}, u32[]{:S(2)}) async-start(bf16[2,16,3,2048]{3,0,2,1:T(2,128)(2,1)} %copy.94), calls=%async_computation.2 | async-start | bytes 786432 | tf_op jit(solution)/shard_map/all_to_all | solution.py:201
  264.0 17.8 %all-to-all-start.1 = ((bf16[2,16,3,2048]{3,0,2,1:T(2,128)(2,1)}), bf16[2,16,3,2048]{3,0,2,1:T(2,128)(2,1)S(1)}, u32[]{:S(2)}, u32[]{:S(2)}) async-start(bf16[2,16,3,2048]{3,0,2,1:T(2,128)(2,1)} %bitcast.16), calls=%async_computation.1 | async-start | bytes 786432 | tf_op jit(solution)/shard_map/all_to_all | solution.py:211
  273.4 12.4 %copy-start.36 = (f32[32]{0:T(128)S(1)}, f32[32]{0:T(128)}, u32[]{:S(2)}) copy-start(f32[32]{0:T(128)} %get-tuple-element.5) | copy-start | bytes 388
  273.4 12.5 %copy-start.18 = (f32[1,32,8]{1,2,0:T(8,128)S(1)}, f32[1,32,8]{1,2,0:T(8,128)}, u32[]{:S(2)}) copy-start(f32[1,32,8]{1,2,0:T(8,128)} %get-tuple-element.33) | copy-start | bytes 3076
  281.8 16.4 %copy-start.20 = (s32[256]{0:T(256)S(1)}, s32[256]{0:T(256)}, u32[]{:S(2)}) copy-start(s32[256]{0:T(256)} %copy-done.19) | copy-start | bytes 3076
  281.8 16.5 %copy-start.38 = (pred[256]{0:T(512)(128)(4,1)S(1)}, pred[256]{0:T(512)(128)(4,1)}, u32[]{:S(2)}) copy-start(pred[256]{0:T(512)(128)(4,1)} %copy-done.37) | copy-start | bytes 772
  281.8 15.8 %all-to-all-start.3 = ((bf16[2,16,3,2048]{3,0,2,1:T(2,128)(2,1)}), bf16[2,16,3,2048]{3,0,2,1:T(2,128)(2,1)S(1)}, u32[]{:S(2)}, u32[]{:S(2)}) async-start(bf16[2,16,3,2048]{3,0,2,1:T(2,128)(2,1)} %bitcast.31), calls=%async_computation.3 | async-start | bytes 786432 | tf_op jit(solution)/shard_map/all_to_all | solution.py:211
  285.5 13.3 %copy-start.22 = (s32[256]{0:T(256)S(1)}, s32[256]{0:T(256)}, u32[]{:S(2)}) copy-start(s32[256]{0:T(256)} %copy-done.21) | copy-start | bytes 3076
  285.5 13.3 %copy-start.40 = (pred[256]{0:T(512)(128)(4,1)S(1)}, pred[256]{0:T(512)(128)(4,1)}, u32[]{:S(2)}) copy-start(pred[256]{0:T(512)(128)(4,1)} %copy-done.39) | copy-start | bytes 772
  (31 other events, 114.0 us)
Sparse Core Ops, SparseCore 0:
  21.3 161.2 all-reduce.2
Sparse Core Ops, SparseCore 1:
  40.1 35.5 all-gather.5
  184.8 27.2 all-gather.7
  213.5 44.7 all-gather.3
